TPU v7x, 256 devices: a whole 4x4x8 slice. The times are simulated.
256 devices in a mesh: panel: 4 (over x), front: 64 (over y, z, core).
Axes of the slice: x: 4, y: 4, z: 8, core: 2. Of those that a mesh axis runs over, the one named last changes fastest.
Arguments:
- top_source: bfloat16 [4, 128, 4096], P('panel', None, 'front'), may hold values from -6 to 6
- leaf_source: bfloat16 [4, 128, 589824], P('panel', None, 'front'), may hold values from -6 to 6
- top_inverse: bfloat16 [4, 4096, 4096], P('panel', 'front'), may hold values from -1 to 4
- leaf_inverse: bfloat16 [4, 2304, 256, 256], P('panel', 'front'), may hold values from -1 to 4
- boundary: bfloat16 [4, 2304, 128, 256], P('panel', 'front'), may hold values from -0.09375 to 0.09375
- touch_rows: int32 [4, 2304, 128], P('panel', 'front'), may hold values from 0 to 4095, as said below
- coupling: float32 [4, 4096], P('panel', 'front'), may hold values from 0.3 to 1
Outputs:
- top_field: bfloat16 [4, 128, 4096], P('panel', None, 'front')
- leaf_field: bfloat16 [4, 128, 589824], P('panel', None, 'front')
Inputs may be any that keep to these rules, and one draw needn't show every extreme that they name: `touch_rows`: front index d owns top front rows d * 64 to (d + 1) * 64 - 1; leaf j of a panel touches only rows owned by front indices j // 36 - 1, j // 36 and j // 36 + 1.
All inputs are finite; a program needn't handle non-finite values.
Results may differ from a plain program's by a relative error of at most 0.02.
Values may be sent and summed in bfloat16 or wider, within the bound.
A program may use at most 64 MiB of HBM per device.

v0:
```python
import jax
import jax.numpy as jnp
from jax import lax
from jax.sharding import PartitionSpec as P


def extended(value, sides, width):
    for axis, dim in sides:
        devices, length = (lax.axis_size(axis), value.shape[dim])
        up = [(i, (i + 1) % devices) for i in range(devices - 1)]
        down = [(j, i) for i, j in up]
        last = lax.slice_in_dim(value, length - width, length, axis=dim)
        leading = lax.slice_in_dim(value, 0, width, axis=dim)
        before = lax.ppermute(last, axis, up)
        after = lax.ppermute(leading, axis, down)
        value = jnp.concatenate([before, value, after], axis=dim)
    return value


def passed_along(block, axis, distance):
    devices = range(lax.axis_size(axis))
    route = [(i - distance, i) for i in devices if i - distance in devices]
    return lax.ppermute(block, axis, route)


def leaf_apply(inverse_blocks, vectors):
    return jnp.einsum("jab,sjb->sja", inverse_blocks, vectors, preferred_element_type=jnp.float32)


def top_fold(vectors, inverse_rows):
    return lax.dot_general(
        lax.all_gather(vectors, "front", axis=1, tiled=True),
        inverse_rows,
        (((1,), (1,)), ((), ())),
        preferred_element_type=jnp.float32,
    )


def lift_through(values, local_rows, boundary, leaf_inverse):
    rows_here = values.shape[2]
    window = extended(values, (("front", 2),), rows_here)
    flat_rows = local_rows[0].reshape(-1)
    picked = jnp.take(window[0], flat_rows, axis=1).reshape(
        values.shape[1], local_rows.shape[1], local_rows.shape[2]
    )
    lifted = jnp.einsum(
        "jkb,sjk->sjb", boundary[0], picked, preferred_element_type=jnp.float32
    ).astype(jnp.bfloat16)
    results = [leaf_apply(leaf_inverse[0], lifted)]
    return jnp.stack(results)


def place_wave(finished, fresh, first_row, in_range):
    older = lax.dynamic_slice_in_dim(finished, first_row, fresh.shape[1], 1)
    return lax.dynamic_update_slice_in_dim(
        finished, jnp.where(in_range, fresh, older), first_row, 1
    )


def body(top_source, leaf_source, top_inverse, leaf_inverse, boundary, touch_rows, coupling):
    panels_here = top_source.shape[0]
    sources_all = top_source.shape[1]
    rows_here = top_source.shape[2]
    leaf_count = leaf_inverse.shape[1]
    leaf_size = leaf_inverse.shape[2]
    group_count = lax.axis_size("panel")
    group_rank = lax.axis_index("panel")
    row_offset = lax.axis_index("front") * rows_here
    local_rows = touch_rows - (row_offset - rows_here)
    vectors = leaf_source.reshape(panels_here, sources_all, leaf_count, leaf_size)
    panel_index = 0
    interior_one = leaf_apply(leaf_inverse[panel_index], vectors[panel_index]).astype(jnp.bfloat16)
    pushed = jnp.einsum(
        "jkb,sjb->sjk", boundary[panel_index], interior_one, preferred_element_type=jnp.float32
    )
    window_one = jnp.zeros((sources_all, 3 * rows_here), jnp.float32)
    window_one = window_one.at[:, local_rows[panel_index].reshape(-1)].add(
        pushed.reshape(sources_all, -1)
    )
    interior_list = [interior_one]
    window_list = [window_one]
    interior = jnp.stack(interior_list)
    windows = jnp.stack(window_list)
    from_below = passed_along(
        windows[:, :, 2 * rows_here :].astype(jnp.bfloat16), "front", 1
    ).astype(jnp.float32)
    from_above = passed_along(windows[:, :, :rows_here].astype(jnp.bfloat16), "front", -1).astype(
        jnp.float32
    )
    known_part = windows[:, :, rows_here : 2 * rows_here] + from_below + from_above
    wave_count = 1
    wave_rows = sources_all // wave_count
    turn_count = group_count + wave_count - 1

    def forward_turn(turn_index, carry):
        incoming, top_done = carry
        wave_index = turn_index - group_rank
        in_range = (wave_index >= 0) & (wave_index < wave_count)
        first_row = jnp.clip(wave_index, 0, wave_count - 1) * wave_rows
        previous = incoming
        own_terms = top_source[0].astype(jnp.float32) + coupling[0] * previous.astype(jnp.float32)
        solved = top_fold((own_terms - known_part[0]).astype(jnp.bfloat16), top_inverse[0])
        previous = solved.astype(jnp.bfloat16)
        top_parts = [previous]
        top_done = place_wave(top_done, jnp.stack(top_parts), first_row, in_range)
        outgoing = passed_along(previous, "panel", 1)
        return (outgoing, top_done)

    start_edge = jnp.zeros((wave_rows, rows_here), jnp.bfloat16)
    unused_edge, forward_tops = lax.fori_loop(
        0, turn_count, forward_turn, (start_edge, jnp.zeros_like(top_source))
    )

    def backward_turn(turn_index, carry):
        incoming, top_done, fixes_done = carry
        wave_index = turn_index - (group_count - 1 - group_rank)
        in_range = (wave_index >= 0) & (wave_index < wave_count)
        first_row = jnp.clip(wave_index, 0, wave_count - 1) * wave_rows
        arriving = incoming
        top_parts = [None] * panels_here
        fix_parts = [None] * panels_here
        for panel_index in reversed(range(panels_here)):
            correction = top_fold(arriving, top_inverse[panel_index]).astype(jnp.bfloat16)
            top_new = (
                forward_tops[panel_index].astype(jnp.float32) + correction.astype(jnp.float32)
            ).astype(jnp.bfloat16)
            top_parts[panel_index] = top_new
            fix_parts[panel_index] = correction
            arriving = (coupling[panel_index] * top_new.astype(jnp.float32)).astype(jnp.bfloat16)
        top_done = place_wave(top_done, jnp.stack(top_parts), first_row, in_range)
        fixes_done = place_wave(fixes_done, jnp.stack(fix_parts), first_row, in_range)
        outgoing = passed_along(arriving, "panel", -1)
        return (outgoing, top_done, fixes_done)

    backward_state = (start_edge, jnp.zeros_like(top_source), jnp.zeros_like(top_source))
    final_edge, top_field, corrections = lax.fori_loop(0, turn_count, backward_turn, backward_state)
    forward_leaf = (
        interior.astype(jnp.float32)
        - lift_through(forward_tops, local_rows, boundary, leaf_inverse)
    ).astype(jnp.bfloat16)
    leaf_field = (
        forward_leaf.astype(jnp.float32)
        - lift_through(corrections, local_rows, boundary, leaf_inverse)
    ).astype(jnp.bfloat16)
    return (top_field, leaf_field.reshape(panels_here, sources_all, -1))


def solution(mesh):
    placed = (
        P("panel", None, "front"),
        P("panel", None, "front"),
        P("panel", "front", None),
        P("panel", "front", None, None),
        P("panel", "front", None, None),
        P("panel", "front", None),
        P("panel", "front"),
    )
    return jax.shard_map(
        body,
        mesh=mesh,
        in_specs=placed,
        out_specs=(P("panel", None, "front"), P("panel", None, "front")),
        check_vma=False,
    )
```

profile of v0, /device:TPU:1, one launch (start us, length us, event | category | flops | bytes accessed | tf_op | source)
XLA Modules:
  0.0 814.4 jit_solution(17682458878577789062)
XLA Ops:
  7.2 4.4 copy.10
  11.7 4.7 fusion.32
  16.5 2.2 fusion.19
  18.7 25.4 %scatter_custom_fusion = f32[128,192]{0,1:T(8,128)S(1)} fusion(s32[4608]{0:T(1024)S(1)} %fusion.44, f32[4608,128]{1,0:T(8,128)} %bitcast.136, f32[]{:T(128)} %constant.79.clone.1), kind=kCustom, calls=%fused_computation.44 | custom fusion | flops 589824 | bytes 98816 | tf_op jit(solution)/shard_map/scatter-add | solution.py:77
  44.1 4.9 collective-permute-start.2
  49.0 1.9 collective-permute-start.3
  51.0 0.6 compare_and_fusion
  51.7 2.4 collective-permute-done.3
  54.2 349.1 %while.36 = (s32[]{:T(128)}, bf16[128,64]{0,1:T(8,128)(2,1)S(1)}, bf16[1,128,64]{1,2,0:T(8,128)(2,1)}, bf16[1,128,64]{1,2,0:T(8,128)(2,1)S(1)}, f32[1,64]{1,0:T(...) while((s32[]{:T(128)}, bf16[128,64]{0,1:T(8,128)(2,1)S(1)}, ...), condition=%wide.region_2.3_spmd.clone, body=%wide.region_1.2_spmd.clone.sunk | while | flops 67182600 | bytes 4964833 | solution.py:110
  54.2 0.7 fusion.55
  54.9 83.0 %all-gather.3.cloned.1.call-done = bf16[128,4096]{0,1:T(8,128)(2,1)} async-done(((bf16[128,64]{0,1:T(8,128)(2,1)}), bf16[128,4096]{0,1:T(8,128)(2,1)}) %all-gather.3.cloned.1.call-update) | async-done | bytes 1048592 | tf_op jit(solution)/shard_map/while/body/eval_jaxpr/all_gather | solution.py:32
  137.9 2.1 bitcast_select_fusion.5
  140.1 3.1 collective-permute-start
  143.2 0.8 collective-permute-done
  144.0 0.7 fusion.55
  144.8 79.7 %all-gather.3.cloned.1.call-done = bf16[128,4096]{0,1:T(8,128)(2,1)} async-done(((bf16[128,64]{0,1:T(8,128)(2,1)}), bf16[128,4096]{0,1:T(8,128)(2,1)}) %all-gather.3.cloned.1.call-update) | async-done | bytes 1048592 | tf_op jit(solution)/shard_map/while/body/eval_jaxpr/all_gather | solution.py:32
  224.4 2.1 bitcast_select_fusion.5
  226.6 3.1 collective-permute-start
  229.7 0.8 collective-permute-done
  230.5 0.7 fusion.55
  231.3 79.7 %all-gather.3.cloned.1.call-done = bf16[128,4096]{0,1:T(8,128)(2,1)} async-done(((bf16[128,64]{0,1:T(8,128)(2,1)}), bf16[128,4096]{0,1:T(8,128)(2,1)}) %all-gather.3.cloned.1.call-update) | async-done | bytes 1048592 | tf_op jit(solution)/shard_map/while/body/eval_jaxpr/all_gather | solution.py:32
  310.9 2.1 bitcast_select_fusion.5
  313.1 3.1 collective-permute-start
  316.2 0.8 collective-permute-done
  317.0 0.7 fusion.55
  317.7 79.4 %all-gather.3.cloned.1.call-done = bf16[128,4096]{0,1:T(8,128)(2,1)} async-done(((bf16[128,64]{0,1:T(8,128)(2,1)}), bf16[128,4096]{0,1:T(8,128)(2,1)}) %all-gather.3.cloned.1.call-update) | async-done | bytes 1048592 | tf_op jit(solution)/shard_map/while/body/eval_jaxpr/all_gather | solution.py:32
  397.1 2.1 bitcast_select_fusion.5
  399.3 3.1 collective-permute-start
  402.4 0.8 collective-permute-done
  403.2 3.0 collective-permute-start.5
  406.3 2.5 collective-permute-start.4
  408.8 343.5 %while.37 = (s32[]{:T(128)}, bf16[128,64]{0,1:T(8,128)(2,1)S(1)}, bf16[1,128,64]{1,2,0:T(8,128)(2,1)S(1)}, bf16[1,128,64]{1,2,0:T(8,128)(2,1)S(1)}, f32[1,64]{1,...) while((s32[]{:T(128)}, bf16[128,64]{0,1:T(8,128)(2,1)S(1)}, ...), condition=%wide.region_4.5_spmd.clone, body=%wide.region_3.4_spmd.clone.sunk | while | flops 67239936 | bytes 5046789 | solution.py:136
  409.5 79.3 %all-gather.5.cloned.1.call-done = bf16[128,4096]{0,1:T(8,128)(2,1)} async-done(((bf16[128,64]{0,1:T(8,128)(2,1)}), bf16[128,4096]{0,1:T(8,128)(2,1)}) %all-gather.5.cloned.1.call-update) | async-done | bytes 1048592 | tf_op jit(solution)/shard_map/while/body/eval_jaxpr/all_gather | solution.py:32
  488.8 1.5 multiply_convert_fusion.2
  490.3 1.3 collective-permute-start.1
  491.6 0.7 bitcast_select_fusion.6
  492.4 2.4 collective-permute-done.1
  494.8 0.6 copy-done.3
  495.5 78.9 %all-gather.5.cloned.1.call-done = bf16[128,4096]{0,1:T(8,128)(2,1)} async-done(((bf16[128,64]{0,1:T(8,128)(2,1)}), bf16[128,4096]{0,1:T(8,128)(2,1)}) %all-gather.5.cloned.1.call-update) | async-done | bytes 1048592 | tf_op jit(solution)/shard_map/while/body/eval_jaxpr/all_gather | solution.py:32
  574.4 1.5 multiply_convert_fusion.2
  575.9 1.3 collective-permute-start.1
  577.2 0.7 bitcast_select_fusion.6
  578.0 2.4 collective-permute-done.1
  580.4 0.6 copy-done.3
  581.2 79.1 %all-gather.5.cloned.1.call-done = bf16[128,4096]{0,1:T(8,128)(2,1)} async-done(((bf16[128,64]{0,1:T(8,128)(2,1)}), bf16[128,4096]{0,1:T(8,128)(2,1)}) %all-gather.5.cloned.1.call-update) | async-done | bytes 1048592 | tf_op jit(solution)/shard_map/while/body/eval_jaxpr/all_gather | solution.py:32
  660.3 1.5 multiply_convert_fusion.2
  661.9 1.3 collective-permute-start.1
  663.2 0.7 bitcast_select_fusion.6
  663.9 2.4 collective-permute-done.1
  667.1 79.1 %all-gather.5.cloned.1.call-done = bf16[128,4096]{0,1:T(8,128)(2,1)} async-done(((bf16[128,64]{0,1:T(8,128)(2,1)}), bf16[128,4096]{0,1:T(8,128)(2,1)}) %all-gather.5.cloned.1.call-update) | async-done | bytes 1048592 | tf_op jit(solution)/shard_map/while/body/eval_jaxpr/all_gather | solution.py:32
  746.3 1.5 multiply_convert_fusion.2
  747.8 1.3 collective-permute-start.1
  749.1 0.7 bitcast_select_fusion.6
  749.8 2.4 collective-permute-done.1
  752.3 3.3 collective-permute-start.7
  755.6 2.2 collective-permute-start.6
  757.9 0.7 maximum_bitcast_fusion
  758.6 10.2 %gather_fusion = bf16[4608,128]{1,0:T(8,128)(2,1)} fusion(bf16[128,192]{0,1:T(8,128)(2,1)S(1)} %maximum_bitcast_fusion, s32[5120]{0:T(1024)S(1)} %pad_clamp_fusion), kind=kCustom, calls=%fused_computation.clone | custom fusion | bytes 2377728 | tf_op jit(solution)/shard_map/jit(_take)/gather | solution.py:43
  768.8 10.2 %gather_fusion.1 = bf16[4608,128]{1,0:T(8,128)(2,1)} fusion(bf16[128,192]{0,1:T(8,128)(2,1)S(1)} %maximum_bitcast_fusion.1, s32[5120]{0:T(1024)S(1)} %pad_clamp_fusion), kind=kCustom, calls=%fused_computation.1.clone | custom fusion | bytes 2377728 | tf_op jit(solution)/shard_map/jit(_take)/gather | solution.py:43
  779.0 4.7 broadcast_select_fusion.1
  783.6 7.2 fusion.7
  790.8 8.2 %fusion.5 = bf16[128,36,256]{2,0,1:T(8,128)(2,1)} fusion(f32[36,128,256]{2,1,0:T(8,128)} %fusion.7, bf16[36,128,256]{2,1,0:T(8,128)(2,1)} %copy-done.2, bf16[1,36,256,256]{3,2,1,0:T(8,128)(2,1)} %param.16, bf16[128,36,128]{0,2,1:T(8,128)(2,1)S(1)} %bitcast.134, bf16[1,36,128,256]{3,2,1,0:T(8,128)(2,1)S(1)} %copy-done), kind=kOutput, calls=%fused_computation.17 | convolution fusion | flops 914227200 | bytes 17694720 | tf_op jit(solution)/shard_map/jab,sjb->sja/dot_general | solution.py:27
  799.0 4.3 copy.12
  803.3 4.3 copy.13
  (56 shorter events, 1.9 us)
Async XLA Ops:
  7.2 9.3 %copy-start = (bf16[1,36,128,256]{3,2,1,0:T(8,128)(2,1)S(1)}, bf16[1,36,128,256]{3,2,1,0:T(8,128)(2,1)}, u32[]{:S(2)}) copy-start(bf16[1,36,128,256]{3,2,1,0:T(8,128)(2,1)} %param.17) | copy-start | bytes 7077892
  7.2 4.4 copy-start.6
  16.4 2.2 copy-start.2
  16.5 37.7 %copy-start.1 = (bf16[1,64,4096]{2,1,0:T(8,128)(2,1)S(1)}, bf16[1,64,4096]{2,1,0:T(8,128)(2,1)}, u32[]{:S(2)}) copy-start(bf16[1,64,4096]{2,1,0:T(8,128)(2,1)} %param.15) | copy-start | bytes 1572868
  16.5 37.7 %copy-start.4 = (bf16[1,128,64]{1,2,0:T(8,128)(2,1)S(1)}, bf16[1,128,64]{1,2,0:T(8,128)(2,1)}, u32[]{:S(2)}) copy-start(bf16[1,128,64]{1,2,0:T(8,128)(2,1)} %param.13) | copy-start | bytes 49156
  16.5 37.7 %copy-start.7 = (f32[1,64]{1,0:T(1,128)S(1)}, f32[1,64]{1,0:T(1,128)}, u32[]{:S(2)}) copy-start(f32[1,64]{1,0:T(1,128)} %param.19) | copy-start | bytes 772
  44.1 7.6 collective-permute-start.2
  49.0 5.1 collective-permute-start.3
  54.2 83.7 %all-gather.3.cloned.1.call-start = ((), (), s32[]{:S(2)}) async-start(), calls=%async_computation | async-start | bytes 1064960 | tf_op jit(solution)/shard_map/while/body/eval_jaxpr/all_gather | solution.py:32
  140.1 3.9 collective-permute-start
  144.0 80.4 %all-gather.3.cloned.1.call-start = ((), (), s32[]{:S(2)}) async-start(), calls=%async_computation | async-start | bytes 1064960 | tf_op jit(solution)/shard_map/while/body/eval_jaxpr/all_gather | solution.py:32
  226.6 3.9 collective-permute-start
  230.5 80.4 %all-gather.3.cloned.1.call-start = ((), (), s32[]{:S(2)}) async-start(), calls=%async_computation | async-start | bytes 1064960 | tf_op jit(solution)/shard_map/while/body/eval_jaxpr/all_gather | solution.py:32
  313.1 3.9 collective-permute-start
  317.0 80.1 %all-gather.3.cloned.1.call-start = ((), (), s32[]{:S(2)}) async-start(), calls=%async_computation | async-start | bytes 1064960 | tf_op jit(solution)/shard_map/while/body/eval_jaxpr/all_gather | solution.py:32
  399.3 3.9 collective-permute-start
  403.2 354.6 %collective-permute-start.5 = (bf16[1,128,64]{1,2,0:T(8,128)(2,1)}, bf16[1,128,64]{1,2,0:T(8,128)(2,1)S(1)}, u32[]{:S(2)}, u32[]{:S(2)}) collective-permute-start(bf16[1,128,64]{1,2,0:T(8,128)(2,1)} %get-tuple-element.580), channel_id=1, source_target_pairs={{1,0},{2,1},{3,2},{4,3},{5,4},{6,5},{7,6},{8,7},{9,8},{10,9},{11,1... | collective-permute-start | bytes 49160 | tf_op jit(solution)/shard_map/ppermute | solution.py:15
  406.3 351.6 %collective-permute-start.4 = (bf16[1,128,64]{1,2,0:T(8,128)(2,1)}, bf16[1,128,64]{1,2,0:T(8,128)(2,1)S(1)}, u32[]{:S(2)}, u32[]{:S(2)}) collective-permute-start(bf16[1,128,64]{1,2,0:T(8,128)(2,1)} %get-tuple-element.580), channel_id=1, source_target_pairs={{0,1},{1,2},{2,3},{3,4},{4,5},{5,6},{6,7},{7,8},{8,9},{9,10},{10,1... | collective-permute-start | bytes 49160 | tf_op jit(solution)/shard_map/ppermute | solution.py:14
  408.8 0.6 copy-start.3
  408.8 80.0 %all-gather.5.cloned.1.call-start = ((), (), s32[]{:S(2)}) async-start(), calls=%async_computation.1 | async-start | bytes 1064960 | tf_op jit(solution)/shard_map/while/body/eval_jaxpr/all_gather | solution.py:32
  490.3 4.5 collective-permute-start.1
  494.8 0.6 copy-start.3
  494.8 79.6 %all-gather.5.cloned.1.call-start = ((), (), s32[]{:S(2)}) async-start(), calls=%async_computation.1 | async-start | bytes 1064960 | tf_op jit(solution)/shard_map/while/body/eval_jaxpr/all_gather | solution.py:32
  575.9 4.5 collective-permute-start.1
  580.4 0.6 copy-start.3
  580.4 79.9 %all-gather.5.cloned.1.call-start = ((), (), s32[]{:S(2)}) async-start(), calls=%async_computation.1 | async-start | bytes 1064960 | tf_op jit(solution)/shard_map/while/body/eval_jaxpr/all_gather | solution.py:32
  661.9 4.5 collective-permute-start.1
  666.4 0.6 copy-start.3
  666.4 79.9 %all-gather.5.cloned.1.call-start = ((), (), s32[]{:S(2)}) async-start(), calls=%async_computation.1 | async-start | bytes 1064960 | tf_op jit(solution)/shard_map/while/body/eval_jaxpr/all_gather | solution.py:32
  747.8 4.5 collective-permute-start.1
  752.3 16.5 %copy-start.5 = (bf16[1,128,64]{1,2,0:T(8,128)(2,1)}, bf16[1,128,64]{1,2,0:T(8,128)(2,1)S(1)}, u32[]{:S(2)}) copy-start(bf16[1,128,64]{1,2,0:T(8,128)(2,1)S(1)} %get-tuple-element.391) | copy-start | bytes 49156
  752.3 16.5 %collective-permute-start.7 = (bf16[1,128,64]{1,2,0:T(8,128)(2,1)S(1)}, bf16[1,128,64]{1,2,0:T(8,128)(2,1)S(1)}, u32[]{:S(2)}, u32[]{:S(2)}) collective-permute-start(bf16[1,128,64]{1,2,0:T(8,128)(2,1)S(1)} %get-tuple-element.336), channel_id=1, source_target_pairs={{1,0},{2,1},{3,2},{4,3},{5,4},{6,5},{7,6},{8,7},{9,8},{10,9},{11,1... | collective-permute-start | bytes 49160 | tf_op jit(solution)/shard_map/ppermute | solution.py:15
  755.6 13.2 %collective-permute-start.6 = (bf16[1,128,64]{1,2,0:T(8,128)(2,1)S(1)}, bf16[1,128,64]{1,2,0:T(8,128)(2,1)S(1)}, u32[]{:S(2)}, u32[]{:S(2)}) collective-permute-start(bf16[1,128,64]{1,2,0:T(8,128)(2,1)S(1)} %get-tuple-element.336), channel_id=1, source_target_pairs={{0,1},{1,2},{2,3},{3,4},{4,5},{5,6},{6,7},{7,8},{8,9},{9,10},{10,1... | collective-permute-start | bytes 49160 | tf_op jit(solution)/shard_map/ppermute | solution.py:14
  768.8 10.2 %copy-start.8 = (pred[4608]{0:T(1024)(128)(4,1)S(1)}, pred[4608]{0:T(1024)(128)(4,1)}, u32[]{:S(2)}) copy-start(pred[4608]{0:T(1024)(128)(4,1)} %compare_and_fusion) | copy-start | bytes 13828
Sparse Core Ops, SparseCore 0:
  58.3 79.5 all-gather.2
  148.2 76.2 all-gather.2
  234.7 76.2 all-gather.2
  320.9 76.2 all-gather.2
  412.7 76.0 all-gather.4
  498.7 75.6 all-gather.4
  584.6 75.6 all-gather.4
  670.5 75.6 all-gather.4
where the time goes:
time: 816 us; the launch traced here: 814 us
  waiting for transfers between devices  654 us (80%)
  other arithmetic  37.2 us (5%)
  matrix products  37.1 us (5%)
  local copies, waits for them, and re-layouts  35.7 us (4%)
  starting transfers between devices  35.5 us (4%)
  between operations  14.3 us (2%)
    all_gather x8, waiting for transfers between devices, top_fold(): lax.all_gather(vectors, 'front', axis=1, tiled=True)  638 us
    scatter-add x1, other arithmetic, body(): window_one.at[:, local_rows[panel_index].reshape(-1)]  25.4 us
    ppermute x10, starting transfers between devices, passed_along(): return lax.ppermute(block, axis, route)  24.3 us
    gather x2, local copies, waits for them, and re-layouts, lift_through(): jnp.take(window[0], flat_rows, axis=1)  20.3 us
    dot_general x3, matrix products, leaf_apply(): jnp.einsum('jab,sjb->sja', inverse_blocks, vectors, preferred_element_typ...  20.1 us
  transfers between devices with their start and end apart: 22, of which 17 were waited for; matrix products, arithmetic and copies ran while one was open for 3% of the time, Pallas kernels for 0%

commit v1 on v0

--- a/solution.py
+++ b/solution.py
@@ -2,6 +2,7 @@
 import jax.numpy as jnp
 from jax import lax
 from jax.sharding import PartitionSpec as P
+from jax.lax import all_to_all, psum
 
 
 def extended(value, sides, width):
@@ -28,8 +29,11 @@
 
 
 def top_fold(vectors, inverse_rows):
+    carry_members_all_in = lambda chunk, a_name: jnp.concatenate(
+        all_to_all(jnp.stack([chunk] * psum(1, a_name), axis=0), a_name, 0, 0), axis=1
+    )
     return lax.dot_general(
-        lax.all_gather(vectors, "front", axis=1, tiled=True),
+        carry_members_all_in(vectors, "front"),
         inverse_rows,
         (((1,), (1,)), ((), ())),
         preferred_element_type=jnp.float32,

time: 816 us -> 460 us (0.56)
  waiting for transfers between devices: 654 us -> 245 us
  starting transfers between devices: 35.5 us -> 98.5 us
  between operations: 14.3 us -> 0.89 us
    all_gather x8 -> x0, waiting for transfers between devices: 638 us -> none  [top_fold(): lax.all_gather(vectors, 'front', axis=1, tiled=True)]
    all_to_all x0 -> x8, waiting for transfers between devices: none -> 228 us  [top_fold(): all_to_all(jnp.stack([chunk] * psum(1, a_name), axis=0), a_name, 0, 0)]
    all_to_all x0 -> x8, starting transfers between devices: none -> 60.1 us  [top_fold(): all_to_all(jnp.stack([chunk] * psum(1, a_name), axis=0), a_name, 0, 0)]
    another operation x0 -> x8, local copies, waits for them, and re-layouts: none -> 9.79 us  [top_fold(): jnp.stack([chunk] * psum(1, a_name), axis=0)]
  transfers between devices with their start and end apart: 22 -> 22, of which waited for: 17 -> 17; matrix products, arithmetic and copies ran while one was open for 3% -> 5% of each run, Pallas kernels for 0% -> 0%
where the time goes in v1:
time: 460 us; the launch traced here: 458 us
  waiting for transfers between devices  245 us (53%)
  starting transfers between devices  98.5 us (21%)
  local copies, waits for them, and re-layouts  43.1 us (9%)
  matrix products  35.6 us (8%)
  other arithmetic  34.8 us (8%)
    all_to_all x8, waiting for transfers between devices, top_fold(): all_to_all(jnp.stack([chunk] * psum(1, a_name), axis=0), a_name, 0, 0)  228 us
    all_to_all x8, starting transfers between devices, top_fold(): all_to_all(jnp.stack([chunk] * psum(1, a_name), axis=0), a_name, 0, 0)  60.1 us
    ppermute x10, starting transfers between devices, passed_along(): return lax.ppermute(block, axis, route)  26.8 us
    scatter-add x1, other arithmetic, body(): window_one.at[:, local_rows[panel_index].reshape(-1)]  25.4 us
    gather x2, local copies, waits for them, and re-layouts, lift_through(): jnp.take(window[0], flat_rows, axis=1)  20.3 us
    dot_general x3, matrix products, leaf_apply(): jnp.einsum('jab,sjb->sja', inverse_blocks, vectors, preferred_element_typ...  20.1 us
    ppermute x10, waiting for transfers between devices, passed_along(): return lax.ppermute(block, axis, route)  16.6 us
    dot_general x8, matrix products, top_fold(): lax.dot_general(carry_members_all_in(vectors, 'front'), inverse_rows, (((...  13.3 us
  transfers between devices with their start and end apart: 22, of which 17 were waited for; matrix products, arithmetic and copies ran while one was open for 5% of the time, Pallas kernels for 0%

profile of v1, /device:TPU:1, one launch (start us, length us, event | category | flops | bytes accessed | tf_op | source)
XLA Modules:
  0.0 458.0 jit_solution(15172391638993485842)
XLA Ops:
  0.7 4.4 copy.12
  5.1 4.7 %fusion.32 = bf16[36,128,256]{2,1,0:T(8,128)(2,1)S(1)} fusion(bf16[128,36,256]{0,2,1:T(8,128)(2,1)} %bitcast.145, bf16[1,36,256,256]{3,2,1,0:T(8,128)(2,1)} %param.16), kind=kOutput, calls=%fused_computation.37 | convolution fusion | flops 605159424 | bytes 9437184 | tf_op jit(solution)/shard_map/jab,sjb->sja/dot_general | solution.py:28
  9.9 2.2 fusion.19
  12.1 25.4 %scatter_custom_fusion = f32[128,192]{0,1:T(8,128)S(1)} fusion(s32[4608]{0:T(1024)S(1)} %fusion.44, f32[4608,128]{1,0:T(8,128)} %bitcast.148, f32[]{:T(128)} %constant.79.clone.1), kind=kCustom, calls=%fused_computation.44 | custom fusion | flops 589824 | bytes 98816 | tf_op jit(solution)/shard_map/scatter-add | solution.py:81
  37.6 4.9 %collective-permute-start.2 = (bf16[1,128,64]{1,2,0:T(8,128)(2,1)S(1)}, bf16[1,128,64]{1,2,0:T(8,128)(2,1)S(1)}, u32[]{:S(2)}, u32[]{:S(2)}) collective-permute-start(bf16[1,128,64]{1,2,0:T(8,128)(2,1)S(1)} %get-tuple-element.431), channel_id=1, source_target_pairs={{0,1},{1,2},{2,3},{3,4},{4,5},{5,6},{6,7},{7,8},{8,9},{9,10},{10,1... | collective-permute-start | bytes 49160 | tf_op jit(solution)/shard_map/ppermute | solution.py:24
  42.5 1.9 collective-permute-start.3
  45.2 2.4 collective-permute-done.3
  47.6 178.3 %while.36 = (s32[]{:T(128)}, bf16[128,64]{0,1:T(8,128)(2,1)S(1)}, bf16[1,128,64]{1,2,0:T(8,128)(2,1)}, bf16[1,128,64]{1,2,0:T(8,128)(2,1)S(1)}, f32[1,64]{1,0:T(...) while((s32[]{:T(128)}, bf16[128,64]{0,1:T(8,128)(2,1)S(1)}, ...), condition=%wide.region_2.3_spmd.clone, body=%wide.region_1.2_spmd.clone.sunk | while | flops 67182600 | bytes 5980633 | solution.py:114
  47.7 1.2 stack.44
  48.9 11.6 %all-to-all-start = ((bf16[64,128,64]{1,2,0:T(8,128)(2,1)}), bf16[64,128,64]{1,2,0:T(8,128)(2,1)S(1)}, u32[]{:S(2)}, u32[]{:S(2)}) async-start(bf16[64,128,64]{1,2,0:T(8,128)(2,1)} %stack.44), calls=%async_computation | async-start | bytes 2097152 | tf_op jit(solution)/shard_map/while/body/eval_jaxpr/all_to_all | solution.py:33
  60.6 28.5 %all-to-all-done = bf16[64,128,64]{1,2,0:T(8,128)(2,1)S(1)} async-done(((bf16[64,128,64]{1,2,0:T(8,128)(2,1)}), bf16[64,128,64]{1,2,0:T(8,128)(2,1)S(1)}, u32[]{:S(2)}, u32[]{:S(2)}) %all-to-all-start) | async-done | bytes 1048608 | tf_op jit(solution)/shard_map/while/body/eval_jaxpr/all_to_all | solution.py:33
  89.1 2.0 bitcast_select_fusion.5
  91.0 3.1 collective-permute-start
  95.1 1.2 stack.44
  96.3 7.1 %all-to-all-start = ((bf16[64,128,64]{1,2,0:T(8,128)(2,1)}), bf16[64,128,64]{1,2,0:T(8,128)(2,1)S(1)}, u32[]{:S(2)}, u32[]{:S(2)}) async-start(bf16[64,128,64]{1,2,0:T(8,128)(2,1)} %stack.44), calls=%async_computation | async-start | bytes 2097152 | tf_op jit(solution)/shard_map/while/body/eval_jaxpr/all_to_all | solution.py:33
  103.4 28.5 %all-to-all-done = bf16[64,128,64]{1,2,0:T(8,128)(2,1)S(1)} async-done(((bf16[64,128,64]{1,2,0:T(8,128)(2,1)}), bf16[64,128,64]{1,2,0:T(8,128)(2,1)S(1)}, u32[]{:S(2)}, u32[]{:S(2)}) %all-to-all-start) | async-done | bytes 1048608 | tf_op jit(solution)/shard_map/while/body/eval_jaxpr/all_to_all | solution.py:33
  131.9 2.0 bitcast_select_fusion.5
  133.9 3.9 collective-permute-start
  138.7 1.2 stack.44
  139.9 7.1 %all-to-all-start = ((bf16[64,128,64]{1,2,0:T(8,128)(2,1)}), bf16[64,128,64]{1,2,0:T(8,128)(2,1)S(1)}, u32[]{:S(2)}, u32[]{:S(2)}) async-start(bf16[64,128,64]{1,2,0:T(8,128)(2,1)} %stack.44), calls=%async_computation | async-start | bytes 2097152 | tf_op jit(solution)/shard_map/while/body/eval_jaxpr/all_to_all | solution.py:33
  147.0 28.5 %all-to-all-done = bf16[64,128,64]{1,2,0:T(8,128)(2,1)S(1)} async-done(((bf16[64,128,64]{1,2,0:T(8,128)(2,1)}), bf16[64,128,64]{1,2,0:T(8,128)(2,1)S(1)}, u32[]{:S(2)}, u32[]{:S(2)}) %all-to-all-start) | async-done | bytes 1048608 | tf_op jit(solution)/shard_map/while/body/eval_jaxpr/all_to_all | solution.py:33
  175.5 2.0 bitcast_select_fusion.5
  177.5 3.9 collective-permute-start
  182.3 1.2 stack.44
  183.6 7.1 %all-to-all-start = ((bf16[64,128,64]{1,2,0:T(8,128)(2,1)}), bf16[64,128,64]{1,2,0:T(8,128)(2,1)S(1)}, u32[]{:S(2)}, u32[]{:S(2)}) async-start(bf16[64,128,64]{1,2,0:T(8,128)(2,1)} %stack.44), calls=%async_computation | async-start | bytes 2097152 | tf_op jit(solution)/shard_map/while/body/eval_jaxpr/all_to_all | solution.py:33
  190.6 28.5 %all-to-all-done = bf16[64,128,64]{1,2,0:T(8,128)(2,1)S(1)} async-done(((bf16[64,128,64]{1,2,0:T(8,128)(2,1)}), bf16[64,128,64]{1,2,0:T(8,128)(2,1)S(1)}, u32[]{:S(2)}, u32[]{:S(2)}) %all-to-all-start) | async-done | bytes 1048608 | tf_op jit(solution)/shard_map/while/body/eval_jaxpr/all_to_all | solution.py:33
  219.1 2.0 bitcast_select_fusion.5
  221.1 3.9 collective-permute-start
  225.9 2.8 collective-permute-start.5
  228.7 2.8 collective-permute-start.4
  231.5 170.8 %while.37 = (s32[]{:T(128)}, bf16[128,64]{0,1:T(8,128)(2,1)S(1)}, bf16[1,128,64]{1,2,0:T(8,128)(2,1)S(1)}, bf16[1,128,64]{1,2,0:T(8,128)(2,1)S(1)}, f32[1,64]{1,...) while((s32[]{:T(128)}, bf16[128,64]{0,1:T(8,128)(2,1)S(1)}, ...), condition=%wide.region_4.5_spmd.clone, body=%wide.region_3.4_spmd.clone.sunk | while | flops 67239936 | bytes 5997025 | solution.py:140
  231.6 1.2 stack.45
  232.8 6.1 %all-to-all-start.1 = ((bf16[64,128,64]{1,2,0:T(8,128)(2,1)}), bf16[64,128,64]{1,2,0:T(8,128)(2,1)S(1)}, u32[]{:S(2)}, u32[]{:S(2)}) async-start(bf16[64,128,64]{1,2,0:T(8,128)(2,1)} %stack.45), calls=%async_computation.1 | async-start | bytes 2097152 | tf_op jit(solution)/shard_map/while/body/eval_jaxpr/all_to_all | solution.py:33
  238.9 28.5 %all-to-all-done.1 = bf16[64,128,64]{1,2,0:T(8,128)(2,1)S(1)} async-done(((bf16[64,128,64]{1,2,0:T(8,128)(2,1)}), bf16[64,128,64]{1,2,0:T(8,128)(2,1)S(1)}, u32[]{:S(2)}, u32[]{:S(2)}) %all-to-all-start.1) | async-done | bytes 1048608 | tf_op jit(solution)/shard_map/while/body/eval_jaxpr/all_to_all | solution.py:33
  267.4 1.4 multiply_convert_fusion.2
  268.8 1.3 collective-permute-start.1
  270.8 2.7 collective-permute-done.1
  273.5 1.2 stack.45
  274.7 7.1 %all-to-all-start.1 = ((bf16[64,128,64]{1,2,0:T(8,128)(2,1)}), bf16[64,128,64]{1,2,0:T(8,128)(2,1)S(1)}, u32[]{:S(2)}, u32[]{:S(2)}) async-start(bf16[64,128,64]{1,2,0:T(8,128)(2,1)} %stack.45), calls=%async_computation.1 | async-start | bytes 2097152 | tf_op jit(solution)/shard_map/while/body/eval_jaxpr/all_to_all | solution.py:33
  281.9 28.5 %all-to-all-done.1 = bf16[64,128,64]{1,2,0:T(8,128)(2,1)S(1)} async-done(((bf16[64,128,64]{1,2,0:T(8,128)(2,1)}), bf16[64,128,64]{1,2,0:T(8,128)(2,1)S(1)}, u32[]{:S(2)}, u32[]{:S(2)}) %all-to-all-start.1) | async-done | bytes 1048608 | tf_op jit(solution)/shard_map/while/body/eval_jaxpr/all_to_all | solution.py:33
  310.4 1.4 multiply_convert_fusion.2
  311.7 1.3 collective-permute-start.1
  313.8 2.7 collective-permute-done.1
  316.5 1.2 stack.45
  317.7 7.1 %all-to-all-start.1 = ((bf16[64,128,64]{1,2,0:T(8,128)(2,1)}), bf16[64,128,64]{1,2,0:T(8,128)(2,1)S(1)}, u32[]{:S(2)}, u32[]{:S(2)}) async-start(bf16[64,128,64]{1,2,0:T(8,128)(2,1)} %stack.45), calls=%async_computation.1 | async-start | bytes 2097152 | tf_op jit(solution)/shard_map/while/body/eval_jaxpr/all_to_all | solution.py:33
  324.8 28.5 %all-to-all-done.1 = bf16[64,128,64]{1,2,0:T(8,128)(2,1)S(1)} async-done(((bf16[64,128,64]{1,2,0:T(8,128)(2,1)}), bf16[64,128,64]{1,2,0:T(8,128)(2,1)S(1)}, u32[]{:S(2)}, u32[]{:S(2)}) %all-to-all-start.1) | async-done | bytes 1048608 | tf_op jit(solution)/shard_map/while/body/eval_jaxpr/all_to_all | solution.py:33
  353.3 1.4 multiply_convert_fusion.2
  354.7 1.3 collective-permute-start.1
  356.7 2.7 collective-permute-done.1
  359.4 1.2 stack.45
  360.6 7.1 %all-to-all-start.1 = ((bf16[64,128,64]{1,2,0:T(8,128)(2,1)}), bf16[64,128,64]{1,2,0:T(8,128)(2,1)S(1)}, u32[]{:S(2)}, u32[]{:S(2)}) async-start(bf16[64,128,64]{1,2,0:T(8,128)(2,1)} %stack.45), calls=%async_computation.1 | async-start | bytes 2097152 | tf_op jit(solution)/shard_map/while/body/eval_jaxpr/all_to_all | solution.py:33
  367.8 28.5 %all-to-all-done.1 = bf16[64,128,64]{1,2,0:T(8,128)(2,1)S(1)} async-done(((bf16[64,128,64]{1,2,0:T(8,128)(2,1)}), bf16[64,128,64]{1,2,0:T(8,128)(2,1)S(1)}, u32[]{:S(2)}, u32[]{:S(2)}) %all-to-all-start.1) | async-done | bytes 1048608 | tf_op jit(solution)/shard_map/while/body/eval_jaxpr/all_to_all | solution.py:33
  396.3 1.4 multiply_convert_fusion.2
  397.6 1.3 collective-permute-start.1
  399.7 2.7 collective-permute-done.1
  402.4 2.9 collective-permute-start.7
  405.2 3.0 collective-permute-start.6
  409.0 10.2 %gather_fusion = bf16[4608,128]{1,0:T(8,128)(2,1)} fusion(bf16[128,192]{0,1:T(8,128)(2,1)S(1)} %maximum_bitcast_fusion, s32[5120]{0:T(1024)S(1)} %pad_clamp_fusion), kind=kCustom, calls=%fused_computation.clone | custom fusion | bytes 2377728 | tf_op jit(solution)/shard_map/jit(_take)/gather | solution.py:47
  419.2 10.2 %gather_fusion.1 = bf16[4608,128]{1,0:T(8,128)(2,1)} fusion(bf16[128,192]{0,1:T(8,128)(2,1)S(1)} %maximum_bitcast_fusion.1, s32[5120]{0:T(1024)S(1)} %pad_clamp_fusion), kind=kCustom, calls=%fused_computation.1.clone | custom fusion | bytes 2377728 | tf_op jit(solution)/shard_map/jit(_take)/gather | solution.py:47
  429.4 4.7 %broadcast_select_fusion.1 = (bf16[4608,128]{1,0:T(8,128)(2,1)S(1)}, bf16[4608,128]{1,0:T(8,128)(2,1)}) fusion(bf16[4608,128]{1,0:T(8,128)(2,1)} %gather_fusion, pred[4608]{0:T(1024)(128)(4,1)S(1)} %copy-done.6, bf16[4608,128]{1,0:T(8,128)(2,1)} %gather_fusion.1), kind=kLoop, calls=%fused_computation.39 | loop fusion | flops 1179648 | bytes 4723200 | tf_op jit(solution)/shard_map/jit(_take)/select_n | solution.py:47
  434.0 7.2 %fusion.7 = f32[36,128,256]{2,1,0:T(8,128)} fusion(bf16[1,36,256,256]{3,2,1,0:T(8,128)(2,1)} %param.16, bf16[128,36,128]{0,2,1:T(8,128)(2,1)} %bitcast.147, bf16[1,36,128,256]{3,2,1,0:T(8,128)(2,1)S(1)} %copy-done), kind=kOutput, calls=%fused_computation.20 | convolution fusion | flops 907149312 | bytes 12976128 | tf_op jit(solution)/shard_map/jab,sjb->sja/dot_general | solution.py:28
  441.2 8.2 %fusion.5 = bf16[128,36,256]{2,0,1:T(8,128)(2,1)} fusion(f32[36,128,256]{2,1,0:T(8,128)} %fusion.7, bf16[36,128,256]{2,1,0:T(8,128)(2,1)} %copy-done.1, bf16[1,36,256,256]{3,2,1,0:T(8,128)(2,1)} %param.16, bf16[128,36,128]{0,2,1:T(8,128)(2,1)S(1)} %bitcast.146, bf16[1,36,128,256]{3,2,1,0:T(8,128)(2,1)S(1)} %copy-done), kind=kOutput, calls=%fused_computation.17 | convolution fusion | flops 914227200 | bytes 17694720 | tf_op jit(solution)/shard_map/jab,sjb->sja/dot_general | solution.py:28
  449.4 4.3 copy.14
  453.7 4.3 copy.15
  (46 shorter events, 8.2 us)
Async XLA Ops:
  0.6 9.3 %copy-start = (bf16[1,36,128,256]{3,2,1,0:T(8,128)(2,1)S(1)}, bf16[1,36,128,256]{3,2,1,0:T(8,128)(2,1)}, u32[]{:S(2)}) copy-start(bf16[1,36,128,256]{3,2,1,0:T(8,128)(2,1)} %param.17) | copy-start | bytes 7077892
  0.6 4.4 copy-start.4
  9.9 2.2 copy-start.1
  9.9 37.7 %copy-start.2 = (bf16[1,128,64]{1,2,0:T(8,128)(2,1)S(1)}, bf16[1,128,64]{1,2,0:T(8,128)(2,1)}, u32[]{:S(2)}) copy-start(bf16[1,128,64]{1,2,0:T(8,128)(2,1)} %param.13) | copy-start | bytes 49156
  9.9 37.7 %copy-start.5 = (f32[1,64]{1,0:T(1,128)S(1)}, f32[1,64]{1,0:T(1,128)}, u32[]{:S(2)}) copy-start(f32[1,64]{1,0:T(1,128)} %param.19) | copy-start | bytes 772
  37.6 7.6 %collective-permute-start.2 = (bf16[1,128,64]{1,2,0:T(8,128)(2,1)S(1)}, bf16[1,128,64]{1,2,0:T(8,128)(2,1)S(1)}, u32[]{:S(2)}, u32[]{:S(2)}) collective-permute-start(bf16[1,128,64]{1,2,0:T(8,128)(2,1)S(1)} %get-tuple-element.431), channel_id=1, source_target_pairs={{0,1},{1,2},{2,3},{3,4},{4,5},{5,6},{6,7},{7,8},{8,9},{9,10},{10,1... | collective-permute-start | bytes 49160 | tf_op jit(solution)/shard_map/ppermute | solution.py:24
  42.5 5.1 %collective-permute-start.3 = (bf16[1,128,64]{1,2,0:T(8,128)(2,1)S(1)}, bf16[1,128,64]{1,2,0:T(8,128)(2,1)S(1)}, u32[]{:S(2)}, u32[]{:S(2)}) collective-permute-start(bf16[1,128,64]{1,2,0:T(8,128)(2,1)S(1)} %get-tuple-element.432), channel_id=1, source_target_pairs={{1,0},{2,1},{3,2},{4,3},{5,4},{6,5},{7,6},{8,7},{9,8},{10,9},{11,1... | collective-permute-start | bytes 49160 | tf_op jit(solution)/shard_map/ppermute | solution.py:24
  48.9 40.2 %all-to-all-start = ((bf16[64,128,64]{1,2,0:T(8,128)(2,1)}), bf16[64,128,64]{1,2,0:T(8,128)(2,1)S(1)}, u32[]{:S(2)}, u32[]{:S(2)}) async-start(bf16[64,128,64]{1,2,0:T(8,128)(2,1)} %stack.44), calls=%async_computation | async-start | bytes 2097152 | tf_op jit(solution)/shard_map/while/body/eval_jaxpr/all_to_all | solution.py:33
  91.0 4.0 collective-permute-start
  96.3 35.6 %all-to-all-start = ((bf16[64,128,64]{1,2,0:T(8,128)(2,1)}), bf16[64,128,64]{1,2,0:T(8,128)(2,1)S(1)}, u32[]{:S(2)}, u32[]{:S(2)}) async-start(bf16[64,128,64]{1,2,0:T(8,128)(2,1)} %stack.44), calls=%async_computation | async-start | bytes 2097152 | tf_op jit(solution)/shard_map/while/body/eval_jaxpr/all_to_all | solution.py:33
  133.9 4.8 %collective-permute-start = (bf16[128,64]{0,1:T(8,128)(2,1)S(1)}, bf16[128,64]{0,1:T(8,128)(2,1)S(1)}, u32[]{:S(2)}, u32[]{:S(2)}) collective-permute-start(bf16[128,64]{0,1:T(8,128)(2,1)S(1)} %get-tuple-element.531), channel_id=1, source_target_pairs={{0,64},{64,128},{128,192},{1,65},{65,129},{129,193},{2,66},{66,130... | collective-permute-start | bytes 49160 | tf_op jit(solution)/shard_map/while/body/eval_jaxpr/ppermute | solution.py:24
  139.9 35.6 %all-to-all-start = ((bf16[64,128,64]{1,2,0:T(8,128)(2,1)}), bf16[64,128,64]{1,2,0:T(8,128)(2,1)S(1)}, u32[]{:S(2)}, u32[]{:S(2)}) async-start(bf16[64,128,64]{1,2,0:T(8,128)(2,1)} %stack.44), calls=%async_computation | async-start | bytes 2097152 | tf_op jit(solution)/shard_map/while/body/eval_jaxpr/all_to_all | solution.py:33
  177.5 4.8 %collective-permute-start = (bf16[128,64]{0,1:T(8,128)(2,1)S(1)}, bf16[128,64]{0,1:T(8,128)(2,1)S(1)}, u32[]{:S(2)}, u32[]{:S(2)}) collective-permute-start(bf16[128,64]{0,1:T(8,128)(2,1)S(1)} %get-tuple-element.531), channel_id=1, source_target_pairs={{0,64},{64,128},{128,192},{1,65},{65,129},{129,193},{2,66},{66,130... | collective-permute-start | bytes 49160 | tf_op jit(solution)/shard_map/while/body/eval_jaxpr/ppermute | solution.py:24
  183.6 35.6 %all-to-all-start = ((bf16[64,128,64]{1,2,0:T(8,128)(2,1)}), bf16[64,128,64]{1,2,0:T(8,128)(2,1)S(1)}, u32[]{:S(2)}, u32[]{:S(2)}) async-start(bf16[64,128,64]{1,2,0:T(8,128)(2,1)} %stack.44), calls=%async_computation | async-start | bytes 2097152 | tf_op jit(solution)/shard_map/while/body/eval_jaxpr/all_to_all | solution.py:33
  221.1 4.8 %collective-permute-start = (bf16[128,64]{0,1:T(8,128)(2,1)S(1)}, bf16[128,64]{0,1:T(8,128)(2,1)S(1)}, u32[]{:S(2)}, u32[]{:S(2)}) collective-permute-start(bf16[128,64]{0,1:T(8,128)(2,1)S(1)} %get-tuple-element.531), channel_id=1, source_target_pairs={{0,64},{64,128},{128,192},{1,65},{65,129},{129,193},{2,66},{66,130... | collective-permute-start | bytes 49160 | tf_op jit(solution)/shard_map/while/body/eval_jaxpr/ppermute | solution.py:24
  225.9 182.4 %collective-permute-start.5 = (bf16[1,128,64]{1,2,0:T(8,128)(2,1)}, bf16[1,128,64]{1,2,0:T(8,128)(2,1)S(1)}, u32[]{:S(2)}, u32[]{:S(2)}) collective-permute-start(bf16[1,128,64]{1,2,0:T(8,128)(2,1)} %get-tuple-element.580), channel_id=1, source_target_pairs={{1,0},{2,1},{3,2},{4,3},{5,4},{6,5},{7,6},{8,7},{9,8},{10,9},{11,1... | collective-permute-start | bytes 49160 | tf_op jit(solution)/shard_map/ppermute | solution.py:16
  228.7 179.5 %collective-permute-start.4 = (bf16[1,128,64]{1,2,0:T(8,128)(2,1)}, bf16[1,128,64]{1,2,0:T(8,128)(2,1)S(1)}, u32[]{:S(2)}, u32[]{:S(2)}) collective-permute-start(bf16[1,128,64]{1,2,0:T(8,128)(2,1)} %get-tuple-element.580), channel_id=1, source_target_pairs={{0,1},{1,2},{2,3},{3,4},{4,5},{5,6},{6,7},{7,8},{8,9},{9,10},{10,1... | collective-permute-start | bytes 49160 | tf_op jit(solution)/shard_map/ppermute | solution.py:15
  232.8 34.6 %all-to-all-start.1 = ((bf16[64,128,64]{1,2,0:T(8,128)(2,1)}), bf16[64,128,64]{1,2,0:T(8,128)(2,1)S(1)}, u32[]{:S(2)}, u32[]{:S(2)}) async-start(bf16[64,128,64]{1,2,0:T(8,128)(2,1)} %stack.45), calls=%async_computation.1 | async-start | bytes 2097152 | tf_op jit(solution)/shard_map/while/body/eval_jaxpr/all_to_all | solution.py:33
  268.8 4.7 %collective-permute-start.1 = (bf16[128,64]{0,1:T(8,128)(2,1)S(1)}, bf16[128,64]{0,1:T(8,128)(2,1)S(1)}, u32[]{:S(2)}, u32[]{:S(2)}) collective-permute-start(bf16[128,64]{0,1:T(8,128)(2,1)S(1)} %get-tuple-element.541), channel_id=1, source_target_pairs={{64,0},{128,64},{192,128},{65,1},{129,65},{193,129},{66,2},{130,66... | collective-permute-start | bytes 49160 | tf_op jit(solution)/shard_map/while/body/eval_jaxpr/ppermute | solution.py:24
  274.7 35.6 %all-to-all-start.1 = ((bf16[64,128,64]{1,2,0:T(8,128)(2,1)}), bf16[64,128,64]{1,2,0:T(8,128)(2,1)S(1)}, u32[]{:S(2)}, u32[]{:S(2)}) async-start(bf16[64,128,64]{1,2,0:T(8,128)(2,1)} %stack.45), calls=%async_computation.1 | async-start | bytes 2097152 | tf_op jit(solution)/shard_map/while/body/eval_jaxpr/all_to_all | solution.py:33
  311.7 4.7 %collective-permute-start.1 = (bf16[128,64]{0,1:T(8,128)(2,1)S(1)}, bf16[128,64]{0,1:T(8,128)(2,1)S(1)}, u32[]{:S(2)}, u32[]{:S(2)}) collective-permute-start(bf16[128,64]{0,1:T(8,128)(2,1)S(1)} %get-tuple-element.541), channel_id=1, source_target_pairs={{64,0},{128,64},{192,128},{65,1},{129,65},{193,129},{66,2},{130,66... | collective-permute-start | bytes 49160 | tf_op jit(solution)/shard_map/while/body/eval_jaxpr/ppermute | solution.py:24
  317.7 35.6 %all-to-all-start.1 = ((bf16[64,128,64]{1,2,0:T(8,128)(2,1)}), bf16[64,128,64]{1,2,0:T(8,128)(2,1)S(1)}, u32[]{:S(2)}, u32[]{:S(2)}) async-start(bf16[64,128,64]{1,2,0:T(8,128)(2,1)} %stack.45), calls=%async_computation.1 | async-start | bytes 2097152 | tf_op jit(solution)/shard_map/while/body/eval_jaxpr/all_to_all | solution.py:33
  354.7 4.7 %collective-permute-start.1 = (bf16[128,64]{0,1:T(8,128)(2,1)S(1)}, bf16[128,64]{0,1:T(8,128)(2,1)S(1)}, u32[]{:S(2)}, u32[]{:S(2)}) collective-permute-start(bf16[128,64]{0,1:T(8,128)(2,1)S(1)} %get-tuple-element.541), channel_id=1, source_target_pairs={{64,0},{128,64},{192,128},{65,1},{129,65},{193,129},{66,2},{130,66... | collective-permute-start | bytes 49160 | tf_op jit(solution)/shard_map/while/body/eval_jaxpr/ppermute | solution.py:24
  360.6 35.6 %all-to-all-start.1 = ((bf16[64,128,64]{1,2,0:T(8,128)(2,1)}), bf16[64,128,64]{1,2,0:T(8,128)(2,1)S(1)}, u32[]{:S(2)}, u32[]{:S(2)}) async-start(bf16[64,128,64]{1,2,0:T(8,128)(2,1)} %stack.45), calls=%async_computation.1 | async-start | bytes 2097152 | tf_op jit(solution)/shard_map/while/body/eval_jaxpr/all_to_all | solution.py:33
  397.6 4.7 %collective-permute-start.1 = (bf16[128,64]{0,1:T(8,128)(2,1)S(1)}, bf16[128,64]{0,1:T(8,128)(2,1)S(1)}, u32[]{:S(2)}, u32[]{:S(2)}) collective-permute-start(bf16[128,64]{0,1:T(8,128)(2,1)S(1)} %get-tuple-element.541), channel_id=1, source_target_pairs={{64,0},{128,64},{192,128},{65,1},{129,65},{193,129},{66,2},{130,66... | collective-permute-start | bytes 49160 | tf_op jit(solution)/shard_map/while/body/eval_jaxpr/ppermute | solution.py:24
  402.4 16.8 %copy-start.3 = (bf16[1,128,64]{1,2,0:T(8,128)(2,1)}, bf16[1,128,64]{1,2,0:T(8,128)(2,1)S(1)}, u32[]{:S(2)}) copy-start(bf16[1,128,64]{1,2,0:T(8,128)(2,1)S(1)} %get-tuple-element.391) | copy-start | bytes 49156
  402.4 16.8 %collective-permute-start.7 = (bf16[1,128,64]{1,2,0:T(8,128)(2,1)S(1)}, bf16[1,128,64]{1,2,0:T(8,128)(2,1)S(1)}, u32[]{:S(2)}, u32[]{:S(2)}) collective-permute-start(bf16[1,128,64]{1,2,0:T(8,128)(2,1)S(1)} %get-tuple-element.336), channel_id=1, source_target_pairs={{1,0},{2,1},{3,2},{4,3},{5,4},{6,5},{7,6},{8,7},{9,8},{10,9},{11,1... | collective-permute-start | bytes 49160 | tf_op jit(solution)/shard_map/ppermute | solution.py:16
  405.2 13.9 %collective-permute-start.6 = (bf16[1,128,64]{1,2,0:T(8,128)(2,1)S(1)}, bf16[1,128,64]{1,2,0:T(8,128)(2,1)S(1)}, u32[]{:S(2)}, u32[]{:S(2)}) collective-permute-start(bf16[1,128,64]{1,2,0:T(8,128)(2,1)S(1)} %get-tuple-element.336), channel_id=1, source_target_pairs={{0,1},{1,2},{2,3},{3,4},{4,5},{5,6},{6,7},{7,8},{8,9},{9,10},{10,1... | collective-permute-start | bytes 49160 | tf_op jit(solution)/shard_map/ppermute | solution.py:15
  419.2 10.2 %copy-start.6 = (pred[4608]{0:T(1024)(128)(4,1)S(1)}, pred[4608]{0:T(1024)(128)(4,1)}, u32[]{:S(2)}) copy-start(pred[4608]{0:T(1024)(128)(4,1)} %compare_and_fusion) | copy-start | bytes 13828
